TPU v7x, 256 devices: a whole 4x4x8 slice. The times are simulated.
256 devices in a mesh: segment: 4 (over x), ctx: 32 (over y, z), tp: 2 (over core).
Axes of the slice: x: 4, y: 4, z: 8, core: 2. Of those that a mesh axis runs over, the one named last changes fastest.
Arguments:
- mamba_input: bfloat16 [4, 4096, 8192], P('segment', 'ctx', 'tp'), may hold values from -13 to 13
- mamba_gate: bfloat16 [4, 4096, 8192], P('segment', 'ctx', 'tp'), may hold values from -6 to 6
- step_size: bfloat16 [4, 4096, 128], P('segment', 'ctx', 'tp'), may hold values from 0 to 2, as said below
- state_maps: bfloat16 [4, 4096, 256], P('segment', 'ctx'), may hold values from -3 to 3
- decay_rate: float32 [128], P('tp'), may hold values from 0.5 to 2
- skip_gain: float32 [128], P('tp'), may hold values from 0.5 to 1.5
- norm_gain: float32 [8192], P('tp'), may hold values from 0.1 to 1.9
- queries: bfloat16 [4, 4096, 8192], P('segment', 'ctx', 'tp'), may hold values from -155 to 154
- keys: bfloat16 [4, 4096, 1024], P('segment', 'ctx', 'tp'), may hold values from -5 to 5
- values: bfloat16 [4, 4096, 1024], P('segment', 'ctx', 'tp'), may hold values from -6 to 6
- source_len: int32 [4], P('segment'), may hold values from 1638 to 3685
Outputs:
- mamba_handed: bfloat16 [4, 4096, 8192], P('segment', 'ctx', 'tp')
- attention_handed: bfloat16 [4, 4096, 8192], P('segment', 'ctx', 'tp')
Inputs may be any that keep to these rules, and one draw needn't show every extreme that they name: `step_size`: positive.
All inputs are finite; a program needn't handle non-finite values.
Results may differ from a plain program's by a relative error of at most 0.0095.
Values may be sent and summed in bfloat16 or wider, within the bound.
A program may use at most 320 MiB of HBM per device.

v0:
```python
import math
import jax
import jax.numpy as jnp
from jax import lax
from jax.sharding import PartitionSpec as P

QUERY_HEADS = 64
KEY_VALUE_HEADS = 8
HEAD_WIDTH = 128
NST = 128
EM = 8192
HP = 64
BLOCK_LEN = 128
precise = lax.Precision.HIGHEST


def from_behind(array, axis, by):
    size = lax.axis_size(axis)
    return lax.ppermute(array, axis, [(i, (i + by) % size) for i in range(size)])


def join_states(earlier, later):
    return (earlier[0] + later[0], jnp.exp(later[0])[..., None, None] * earlier[1] + later[1])


def scan_blocks(mixer_in, step_in, maps_in, speed_collection, skips):
    tok_rows = mixer_in.shape[0]
    head_count = step_in.shape[1]
    block_len = min(BLOCK_LEN, tok_rows)
    blocks = tok_rows // block_len
    step_float = step_in.astype(jnp.float32).reshape(blocks, block_len, head_count)
    log_decay = -speed_collection[None, None, :] * step_float
    cum_log = jnp.cumsum(log_decay, axis=1)
    x_float = mixer_in.astype(jnp.float32).reshape(blocks, block_len, head_count, HP)
    b_float = maps_in[:, :NST].astype(jnp.float32).reshape(blocks, block_len, NST)
    c_float = maps_in[:, NST:].astype(jnp.float32).reshape(blocks, block_len, NST)
    gram = jnp.einsum("cin,cjn->cij", c_float, b_float, precision=precise)
    lower_tri = (jnp.arange(block_len)[:, None] >= jnp.arange(block_len)[None, :])[None, :, :, None]
    differ = cum_log[:, :, None, :] - cum_log[:, None, :, :]
    decay = jnp.where(lower_tri, jnp.exp(jnp.where(lower_tri, differ, 0.0)), 0.0)
    weights = gram[..., None] * decay * step_float[:, None, :, :]
    inner_out = jnp.einsum("cijh,cjhp->cihp", weights, x_float, precision=precise)
    tail_decay = jnp.exp(cum_log[:, -1:, :] - cum_log) * step_float
    block_states = jnp.einsum("cjh,cjn,cjhp->chnp", tail_decay, b_float, x_float, precision=precise)
    block_logs = cum_log[:, -1, :]
    inc_logs, inc_states = lax.associative_scan(join_states, (block_logs, block_states), axis=0)
    entering = jnp.concatenate([jnp.zeros_like(block_states[:1]), inc_states[:-1]], axis=0)
    enter_logs = jnp.concatenate([jnp.zeros_like(block_logs[:1]), inc_logs[:-1]], axis=0)
    outer_out = jnp.exp(cum_log)[..., None] * jnp.einsum(
        "cin,chnp->cihp", c_float, entering, precision=precise
    )
    mixed = inner_out + outer_out + skips[None, None, :, None] * x_float
    cum_block = (cum_log + enter_logs[:, None, :]).reshape(tok_rows, head_count)
    return (mixed.reshape(tok_rows, head_count, HP), inc_states[-1], inc_logs[-1], cum_block)


def on_device(
    mamba_input,
    mamba_gate,
    step_size,
    state_maps,
    decay_rate,
    skip_gain,
    norm_gain,
    queries,
    keys,
    values,
    source_len,
):
    mixer_in = mamba_input[0]
    gate_in = mamba_gate[0]
    step_in = step_size[0]
    maps_in = state_maps[0]
    tok_rows = mixer_in.shape[0]
    ctx_index = lax.axis_index("ctx")
    chan_rows, chan_steps = (
        lax.all_to_all(mixer_in, "ctx", split_axis=1, concat_axis=0, tiled=True),
        lax.all_to_all(step_in, "ctx", split_axis=1, concat_axis=0, tiled=True),
    )
    all_maps = lax.all_gather(maps_in, "ctx", axis=0, tiled=True)
    sub_heads = chan_steps.shape[1]
    rate_sub = lax.dynamic_slice_in_dim(decay_rate, ctx_index * sub_heads, sub_heads)
    skip_sub = lax.dynamic_slice_in_dim(skip_gain, ctx_index * sub_heads, sub_heads)
    chan_out, _, _, _ = scan_blocks(chan_rows, chan_steps, all_maps, rate_sub, skip_sub)
    chan_out = chan_out.reshape(chan_rows.shape[0], sub_heads * HP).astype(jnp.bfloat16)
    raw = lax.all_to_all(chan_out, "ctx", split_axis=0, concat_axis=1, tiled=True)
    gated = raw.astype(jnp.float32) * jax.nn.silu(gate_in.astype(jnp.float32))
    square_sums = lax.psum(jnp.sum(gated * gated, axis=-1), "tp")
    mean_sq = square_sums / EM
    mamba_out = (gated * lax.rsqrt(mean_sq + 1e-05)[:, None] * norm_gain[None, :]).astype(
        jnp.bfloat16
    )
    query_in = queries[0]
    kv_local = keys.shape[2] // HEAD_WIDTH
    group_width = QUERY_HEADS // KEY_VALUE_HEADS
    query_head_rows = query_in.reshape(tok_rows, kv_local, group_width, HEAD_WIDTH)
    source = source_len[0]
    query_pos = ctx_index * tok_rows + jnp.arange(tok_rows, dtype=jnp.int32)
    scale = 1.0 / math.sqrt(HEAD_WIDTH)
    start_max = jnp.full((kv_local, group_width, tok_rows), -1e30, jnp.float32)
    key_piece = lax.all_gather(keys[0], "ctx", axis=0, tiled=True)
    value_piece = lax.all_gather(values[0], "ctx", axis=0, tiled=True)
    piece_rows = key_piece.shape[0]
    key_head_rows = key_piece.reshape(piece_rows, kv_local, HEAD_WIDTH)
    value_head_rows = value_piece.reshape(piece_rows, kv_local, HEAD_WIDTH)
    key_pos = jnp.arange(piece_rows, dtype=jnp.int32)
    visible = (key_pos[None, :] <= query_pos[:, None]) | (key_pos[None, :] < source)
    scores = (
        jnp.einsum(
            "tkgd,skd->kgts", query_head_rows, key_head_rows, preferred_element_type=jnp.float32
        )
        * scale
    )
    scores = jnp.where(visible[None, None], scores, -jnp.inf)
    new_max = jnp.maximum(start_max, jnp.max(scores, axis=-1))
    weights = jnp.exp(scores - new_max[..., None])
    new_total = jnp.sum(weights, axis=-1)
    product = jnp.einsum(
        "kgts,skd->kgtd",
        weights.astype(jnp.bfloat16),
        value_head_rows,
        preferred_element_type=jnp.float32,
    )
    attention_out = (
        (product / new_total[..., None])
        .transpose(2, 0, 1, 3)
        .reshape(tok_rows, kv_local * group_width * HEAD_WIDTH)
        .astype(jnp.bfloat16)
    )
    mamba_next, attention_next = from_behind((mamba_out, attention_out), "segment", 1)
    return (mamba_next[None], attention_next[None])


def solution(mesh):
    placed = (
        P("segment", "ctx", "tp"),
        P("segment", "ctx", "tp"),
        P("segment", "ctx", "tp"),
        P("segment", "ctx", None),
        P("tp"),
        P("tp"),
        P("tp"),
        P("segment", "ctx", "tp"),
        P("segment", "ctx", "tp"),
        P("segment", "ctx", "tp"),
        P("segment"),
    )
    return jax.shard_map(
        on_device,
        mesh=mesh,
        in_specs=placed,
        out_specs=(P("segment", "ctx", "tp"), P("segment", "ctx", "tp")),
        check_vma=False,
    )
```

profile of v0, /device:TPU:32, one launch (start us, length us, event | category | flops | bytes accessed | tf_op | source)
XLA Modules:
  0.0 349.6 jit_solution(2937649183413915487)
XLA Ops:
  7.9 11.4 %all-to-all-start = ((bf16[128,32,2]{0,2,1:T(2,128)(2,1)}), bf16[128,32,2]{0,2,1:T(2,128)(2,1)S(1)}, u32[]{:S(2)}, u32[]{:S(2)}) async-start(bf16[128,32,2]{0,2,1:T(2,128)(2,1)} %bitcast.126), calls=%async_computation | async-start | bytes 32768 | tf_op jit(solution)/shard_map/all_to_all | solution.py:78
  22.4 2.3 copy.117
  24.7 3.1 all-to-all-done
  27.8 6.7 %all-to-all-start.1 = ((bf16[128,32,128]{0,2,1:T(8,128)(2,1)}), bf16[128,32,128]{0,2,1:T(8,128)(2,1)S(1)}, u32[]{:S(2)}, u32[]{:S(2)}) async-start(bf16[128,32,128]{0,2,1:T(8,128)(2,1)} %bitcast.5), calls=%async_computation.1 | async-start | bytes 2097152 | tf_op jit(solution)/shard_map/all_to_all | solution.py:77
  34.6 2.8 copy.87
  47.2 3.3 copy.92
  50.9 41.8 %all-gather.7.cloned.1.call-done = bf16[1,4096,256]{2,1,0:T(8,128)(2,1)} async-done(((bf16[1,128,256]{2,1,0:T(8,128)(2,1)}), bf16[1,4096,256]{2,1,0:T(8,128)(2,1)}) %all-gather.7.cloned.1.call-update) | async-done | bytes 2097168 | tf_op jit(solution)/shard_map/all_gather | solution.py:80
  92.7 3.0 fusion.54
  95.7 2.4 fusion.36
  105.4 3.4 pad.35
  110.5 5.1 %pad.37 = f32[8,2,128,64]{2,3,1,0:T(8,128)} pad(f32[4,2,128,64]{2,3,1,0:T(8,128)} %add.123, f32[]{:T(128)} %constant.9.clone.1), padding=1_0_1x0_0_0x0_0_0x0_0_0 | pad | bytes 786436 | tf_op jit(solution)/shard_map/pad | solution.py:46
  116.8 3.2 pad.36
  124.3 9.2 %pad.38 = f32[16,2,128,64]{2,3,1,0:T(8,128)} pad(f32[8,2,128,64]{2,3,1,0:T(8,128)} %pad_maximum_fusion.1, f32[]{:T(128)} %constant.9.clone.1), padding=0_1_1x0_0_0x0_0_0x0_0_0 | pad | bytes 1572868 | tf_op jit(solution)/shard_map/pad | solution.py:46
  133.5 9.2 %pad.39 = f32[16,2,128,64]{2,3,1,0:T(8,128)} pad(f32[8,2,128,64]{2,3,1,0:T(8,128)} %add.125, f32[]{:T(128)} %constant.9.clone.1), padding=1_0_1x0_0_0x0_0_0x0_0_0 | pad | bytes 1572868 | tf_op jit(solution)/shard_map/pad | solution.py:46
  142.7 2.7 add.127
  145.5 16.6 %pad.73 = f32[32,2,128,64]{2,3,1,0:T(8,128)} pad(f32[16,2,128,64]{2,3,1,0:T(8,128)} %add.127, f32[]{:T(128)} %constant.9.clone.1), padding=1_0_1x0_0_0x0_0_0x0_0_0 | pad | bytes 3145732
  164.8 12.4 %pad.51 = f32[31,2,128,64]{2,3,1,0:T(8,128)S(1)} pad(f32[16,2,128,64]{2,3,1,0:T(8,128)} %pad_maximum_fusion, f32[]{:T(128)} %constant.9.clone.1), padding=0_0_1x0_0_0x0_0_0x0_0_0 | pad | bytes 3080196 | tf_op jit(solution)/shard_map/slice | solution.py:47
  177.2 2.4 fusion.62
  179.7 4.9 %fusion.6 = f32[32,2,128,64]{2,3,1,0:T(8,128)S(1)} fusion(bf16[32,128,2,64]{1,3,2,0:T(8,128)(2,1)S(1)} %bitcast.106, f32[32,128,2]{1,2,0:T(2,128)S(1)} %copy-done.9, f32[32,128,2]{1,2,0:T(2,128)S(1)} %copy-done.8, f32[32,128,128]{2,1,0:T(8,128)S(1)} %fusion.62, pred[128,128]{1,0:T(8,128)(4,1)S(1)} %copy-done.11), kind=kOutput, calls=%fused_computation.7 | convolution fusion | flops 810549248 | bytes 5324800 | tf_op jit(solution)/shard_map/cijh,cjhp->cihp/dot_general | solution.py:42
  184.6 3.3 fusion.15
  187.9 7.1 %all-to-all-start.2 = ((bf16[32,128,128]{1,2,0:T(8,128)(2,1)}), bf16[32,128,128]{1,2,0:T(8,128)(2,1)S(1)}, u32[]{:S(2)}, u32[]{:S(2)}) async-start(bf16[32,128,128]{1,2,0:T(8,128)(2,1)} %bitcast.115), calls=%async_computation.2 | async-start | bytes 2097152 | tf_op jit(solution)/shard_map/all_to_all | solution.py:86
  201.7 17.6 %all-to-all-done.2 = bf16[32,128,128]{1,2,0:T(8,128)(2,1)S(1)} async-done(((bf16[32,128,128]{1,2,0:T(8,128)(2,1)}), bf16[32,128,128]{1,2,0:T(8,128)(2,1)S(1)}, u32[]{:S(2)}, u32[]{:S(2)}) %all-to-all-start.2) | async-done | bytes 1048608 | tf_op jit(solution)/shard_map/all_to_all | solution.py:86
  220.9 2.9 copy.118
  223.8 2.3 fusion.24
  226.2 2.5 psum.7
  228.7 2.6 fusion.31
  232.8 26.4 %fusion.2 = (f32[4,8,128]{2,1,0:T(8,128)S(1)}, f32[4,4096,128,8]{2,1,3,0:T(8,128)}) fusion(pred[128,4096]{0,1:T(8,128)(4,1)S(1)} %fusion.32, bf16[4096,4,128,1]{0,2,3,1:T(8,128)(2,1)} %bitcast.116, bf16[128,4,8,128]{3,2,1,0:T(8,128)(2,1)S(1)} %bitcast.114), kind=kOutput, calls=%fused_computation.4 | convolution fusion | flops 4345294848 | bytes 72892416 | tf_op jit(solution)/shard_map/tkgd,skd->kgts/dot_general | solution.py:109
  259.3 21.8 %fusion = f32[4,8,128]{2,1,0:T(8,128)S(1)} fusion(f32[4,4096,128,8]{2,1,3,0:T(8,128)} %get-tuple-element.17, f32[4,8,128]{2,1,0:T(8,128)S(1)} %broadcast_maximum_fusion, pred[128,4096]{0,1:T(8,128)(4,1)S(1)} %fusion.32), kind=kLoop, calls=%fused_computation.2 | loop fusion | flops 67104768 | bytes 67665920 | tf_op jit(solution)/shard_map/reduce_sum | solution.py:117
  281.6 6.4 %copy.109 = bf16[1,4096,512]{1,2,0:T(8,128)(2,1)} copy(bf16[1,4096,512]{2,1,0:T(8,128)(2,1)} %all-gather.11.cloned.1.call-done) | data formatting | bytes 8388608 | tf_op jit(solution)/shard_map/all_gather | solution.py:102
  287.9 25.5 %fusion.16 = bf16[128,4,8,128]{0,3,2,1:T(8,128)(2,1)S(1)} fusion(bf16[4096,4,128,1]{0,2,3,1:T(8,128)(2,1)} %bitcast.117, f32[4,4096,128,8]{2,1,3,0:T(8,128)} %get-tuple-element.17, f32[4,8,128]{2,1,0:T(8,128)S(1)} %broadcast_maximum_fusion, pred[128,4096]{0,1:T(8,128)(4,1)S(1)} %fusion.32, f32[128,4,8]{0,2,1:T(8,128)S(1)} %bitcast.127), kind=kOutput, calls=%fused_computation.20 | convolution fusion | flops 4363124736 | bytes 72908800 | tf_op jit(solution)/shard_map/kgts,skd->kgtd/dot_general | solution.py:118
  315.4 24.3 %collective-permute-done.1 = bf16[128,4096]{1,0:T(8,128)(2,1)S(1)} collective-permute-done((bf16[128,4096]{1,0:T(8,128)(2,1)S(1)}, bf16[128,4096]{1,0:T(8,128)(2,1)S(1)}, u32[]{:S(2)}, u32[]{:S(2)}) %collective-permute-start.1) | collective-permute-done | bytes 1048608 | tf_op jit(solution)/shard_map/ppermute | solution.py:19
  339.8 2.3 copy.133
  (112 shorter events, 43.8 us)
Async XLA Ops:
  7.2 17.5 %copy-start.12 = (f32[64]{0:T(128)S(1)}, f32[64]{0:T(128)}, u32[]{:S(2)}) copy-start(f32[64]{0:T(128)} %param.16) | copy-start | bytes 772
  7.2 85.5 %all-gather.7.cloned.1.call-start = ((), (), s32[]{:S(2)}) async-start(), calls=%async_computation.3 | async-start | bytes 2162688 | tf_op jit(solution)/shard_map/all_gather | solution.py:80
  7.9 19.9 %all-to-all-start = ((bf16[128,32,2]{0,2,1:T(2,128)(2,1)}), bf16[128,32,2]{0,2,1:T(2,128)(2,1)S(1)}, u32[]{:S(2)}, u32[]{:S(2)}) async-start(bf16[128,32,2]{0,2,1:T(2,128)(2,1)} %bitcast.126), calls=%async_computation | async-start | bytes 32768 | tf_op jit(solution)/shard_map/all_to_all | solution.py:78
  19.3 213.5 %all-gather.9.cloned.1.call-start = ((), (), s32[]{:S(2)}) async-start(), calls=%async_computation.4 | async-start | bytes 4325376 | tf_op jit(solution)/shard_map/all_gather | solution.py:101
  27.8 67.9 %all-to-all-start.1 = ((bf16[128,32,128]{0,2,1:T(8,128)(2,1)}), bf16[128,32,128]{0,2,1:T(8,128)(2,1)S(1)}, u32[]{:S(2)}, u32[]{:S(2)}) async-start(bf16[128,32,128]{0,2,1:T(8,128)(2,1)} %bitcast.5), calls=%async_computation.1 | async-start | bytes 2097152 | tf_op jit(solution)/shard_map/all_to_all | solution.py:77
  98.9 1.0 copy-start.2
  100.0 0.8 copy-start.4
  101.1 0.6 copy-start.5
  101.1 15.7 %slice-start.1 = ((f32[8,2,128,64]{2,3,1,0:T(8,128)}), f32[1,2,128,64]{2,3,1,0:T(8,128)S(1)}, s32[]{:S(2)}) async-start(f32[8,2,128,64]{2,3,1,0:T(8,128)} %copy-done.4), calls=%async_computation.7 | async-start | bytes 131072 | tf_op jit(solution)/shard_map/slice | solution.py:46
  116.8 6.7 %slice-start = ((f32[16,2,128,64]{2,3,1,0:T(8,128)}), f32[1,2,128,64]{2,3,1,0:T(8,128)S(1)}, s32[]{:S(2)}) async-start(f32[16,2,128,64]{2,3,1,0:T(8,128)} %copy-done.2), calls=%async_computation.6 | async-start | bytes 131072 | tf_op jit(solution)/shard_map/slice | solution.py:46
  162.0 1.7 copy-start.6
  177.2 2.4 copy-start.8
  177.2 2.4 copy-start.9
  177.2 2.4 copy-start.11
  179.6 5.0 %copy-start = (f32[32,2,128,64]{2,3,1,0:T(8,128)S(1)}, f32[32,2,128,64]{2,3,1,0:T(8,128)}, u32[]{:S(2)}) copy-start(f32[32,2,128,64]{2,3,1,0:T(8,128)} %pad.73) | copy-start | bytes 6291460
  179.6 5.0 %copy-start.1 = (bf16[4096,128]{1,0:T(8,128)(2,1)S(1)}, bf16[4096,128]{1,0:T(8,128)(2,1)}, u32[]{:S(2)}) copy-start(bf16[4096,128]{1,0:T(8,128)(2,1)} %get-tuple-element.3) | copy-start | bytes 3145732
  179.6 5.0 %copy-start.7 = (f32[32,128,2]{1,2,0:T(2,128)S(1)}, f32[32,128,2]{1,2,0:T(2,128)}, u32[]{:S(2)}) copy-start(f32[32,128,2]{1,2,0:T(2,128)} %copy.92) | copy-start | bytes 98308
  187.9 7.9 %copy-start.3 = (bf16[1,128,4096]{2,1,0:T(8,128)(2,1)S(1)}, bf16[1,128,4096]{2,1,0:T(8,128)(2,1)}, u32[]{:S(2)}) copy-start(bf16[1,128,4096]{2,1,0:T(8,128)(2,1)} %param.12) | copy-start | bytes 3145732
  187.9 31.4 %all-to-all-start.2 = ((bf16[32,128,128]{1,2,0:T(8,128)(2,1)}), bf16[32,128,128]{1,2,0:T(8,128)(2,1)S(1)}, u32[]{:S(2)}, u32[]{:S(2)}) async-start(bf16[32,128,128]{1,2,0:T(8,128)(2,1)} %bitcast.115), calls=%async_computation.2 | async-start | bytes 2097152 | tf_op jit(solution)/shard_map/all_to_all | solution.py:86
  195.1 86.5 %all-gather.11.cloned.1.call-start = ((), (), s32[]{:S(2)}) async-start(), calls=%async_computation.5 | async-start | bytes 4325376 | tf_op jit(solution)/shard_map/all_gather | solution.py:102
  223.8 4.8 %copy-start.10 = (f32[4096]{0:T(1024)S(1)}, f32[4096]{0:T(1024)}, u32[]{:S(2)}) copy-start(f32[4096]{0:T(1024)} %param.17) | copy-start | bytes 49156
  231.3 84.2 %collective-permute-start = (bf16[128,4096]{1,0:T(8,128)(2,1)S(1)}, bf16[128,4096]{1,0:T(8,128)(2,1)}, u32[]{:S(2)}, u32[]{:S(2)}) collective-permute-start(bf16[128,4096]{1,0:T(8,128)(2,1)S(1)} %fusion.31), channel_id=1, source_target_pairs={{0,64},{64,128},{128,192},{192,0},{1,65},{65,129},{129,193},{193,1... | collective-permute-start | bytes 3145736 | tf_op jit(solution)/shard_map/ppermute | solution.py:19
  313.9 25.8 %collective-permute-start.1 = (bf16[128,4096]{1,0:T(8,128)(2,1)S(1)}, bf16[128,4096]{1,0:T(8,128)(2,1)S(1)}, u32[]{:S(2)}, u32[]{:S(2)}) collective-permute-start(bf16[128,4096]{1,0:T(8,128)(2,1)S(1)} %copy.111), channel_id=1, source_target_pairs={{0,64},{64,128},{128,192},{192,0},{1,65},{65,129},{129,193},{193,1... | collective-permute-start | bytes 3145736 | tf_op jit(solution)/shard_map/ppermute | solution.py:19
Sparse Core Ops, SparseCore 0:
  10.6 82.0 all-gather.6
  95.2 81.4 all-gather.8
  198.5 83.0 all-gather.10
where the time goes:
time: 356 us; the launch traced here: 350 us
  local copies, waits for them, and re-layouts  101 us (28%)
  waiting for transfers between devices  88.7 us (25%)
  matrix products  64.9 us (18%)
  other arithmetic  49.3 us (14%)
  starting transfers between devices  28.3 us (8%)
  between operations  14.7 us (4%)
    all_gather x1, waiting for transfers between devices, on_device(): all_maps = lax.all_gather(maps_in, 'ctx', axis=0, tiled=True)  41.8 us
    pad x6, local copies, waits for them, and re-layouts, scan_blocks(): lax.associative_scan(join_states, (block_logs, block_states), axis=0)  31.7 us
    dot_general x1, matrix products, on_device(): jnp.einsum('tkgd,skd->kgts', query_head_rows, key_head_rows, preferred_el...  26.4 us
    dot_general x1, matrix products, on_device(): jnp.einsum('kgts,skd->kgtd', weights.astype(jnp.bfloat16), value_head_row...  25.5 us
    unnamed x31, local copies, waits for them, and re-layouts  25.3 us
    ppermute x2, waiting for transfers between devices, from_behind(): lax.ppermute(array, axis, [(i, (i + by) % size) for i in range(size)])  24.3 us
    reduce_sum x1, other arithmetic, on_device(): new_total = jnp.sum(weights, axis=-1)  21.8 us
    all_to_all x1, waiting for transfers between devices, on_device(): lax.all_to_all(chan_out, 'ctx', split_axis=0, concat_axis=1, tiled=True)  17.6 us
  transfers between devices with their start and end apart: 8, of which 5 were waited for; matrix products, arithmetic and copies ran while one was open for 60% of the time, Pallas kernels for 0%

commit v1 on v0

--- a/solution.py
+++ b/solution.py
@@ -3,6 +3,7 @@
 import jax.numpy as jnp
 from jax import lax
 from jax.sharding import PartitionSpec as P
+from jax.lax import all_to_all, axis_size
 
 QUERY_HEADS = 64
 KEY_VALUE_HEADS = 8
@@ -77,7 +78,10 @@
         lax.all_to_all(mixer_in, "ctx", split_axis=1, concat_axis=0, tiled=True),
         lax.all_to_all(step_in, "ctx", split_axis=1, concat_axis=0, tiled=True),
     )
-    all_maps = lax.all_gather(maps_in, "ctx", axis=0, tiled=True)
+    steps_seen = []
+    for _ in range(axis_size("ctx")):
+        steps_seen.append(maps_in)
+    all_maps = jnp.concatenate(all_to_all(jnp.stack(steps_seen), "ctx", 0, 0), axis=0)
     sub_heads = chan_steps.shape[1]
     rate_sub = lax.dynamic_slice_in_dim(decay_rate, ctx_index * sub_heads, sub_heads)
     skip_sub = lax.dynamic_slice_in_dim(skip_gain, ctx_index * sub_heads, sub_heads)

time: 356 us -> 387 us (1.087)
  blocking collectives: 2.46 us -> 22.4 us
  waiting for transfers between devices: 88.7 us -> 108 us
  starting transfers between devices: 28.3 us -> 20.2 us
    all_gather x1 -> x0, waiting for transfers between devices: 41.8 us -> none  [on_device(): all_maps = lax.all_gather(maps_in, 'ctx', axis=0, tiled=True)]
    all_to_all x1, waiting for transfers between devices: 3.13 us -> 44.3 us  [on_device(): all_to_all(jnp.stack(steps_seen), 'ctx', 0, 0)]
    all_to_all x0 -> x1, blocking collectives: none -> 19.9 us  [on_device(): lax.all_to_all(step_in, 'ctx', split_axis=1, concat_axis=0, tiled=True)]
    all_to_all x1, waiting for transfers between devices: 0.01 us -> 19.1 us  [on_device(): lax.all_to_all(mixer_in, 'ctx', split_axis=1, concat_axis=0, tiled=True)]
    all_to_all x1, starting transfers between devices: 11.4 us -> 5.88 us  [on_device(): all_to_all(jnp.stack(steps_seen), 'ctx', 0, 0)]
    unnamed x31 -> x37, local copies, waits for them, and re-layouts: 25.3 us -> 24.4 us
  transfers between devices with their start and end apart: 8 -> 7, of which waited for: 5 -> 4; matrix products, arithmetic and copies ran while one was open for 60% -> 54% of each run, Pallas kernels for 0% -> 0%
where the time goes in v1:
time: 387 us; the launch traced here: 381 us
  waiting for transfers between devices  108 us (28%)
  local copies, waits for them, and re-layouts  102 us (26%)
  matrix products  65 us (17%)
  other arithmetic  48.5 us (13%)
  blocking collectives  22.4 us (6%)
  starting transfers between devices  20.2 us (5%)
  between operations  15.1 us (4%)
    all_to_all x1, waiting for transfers between devices, on_device(): all_to_all(jnp.stack(steps_seen), 'ctx', 0, 0)  44.3 us
    pad x6, local copies, waits for them, and re-layouts, scan_blocks(): lax.associative_scan(join_states, (block_logs, block_states), axis=0)  31.7 us
    dot_general x1, matrix products, on_device(): jnp.einsum('tkgd,skd->kgts', query_head_rows, key_head_rows, preferred_el...  26.5 us
    dot_general x1, matrix products, on_device(): jnp.einsum('kgts,skd->kgtd', weights.astype(jnp.bfloat16), value_head_row...  25.5 us
    ppermute x2, waiting for transfers between devices, from_behind(): lax.ppermute(array, axis, [(i, (i + by) % size) for i in range(size)])  24.9 us
    unnamed x37, local copies, waits for them, and re-layouts  24.4 us
    reduce_sum x1, other arithmetic, on_device(): new_total = jnp.sum(weights, axis=-1)  21.8 us
    all_to_all x1, blocking collectives, on_device(): lax.all_to_all(step_in, 'ctx', split_axis=1, concat_axis=0, tiled=True)  19.9 us
  transfers between devices with their start and end apart: 7, of which 4 were waited for; matrix products, arithmetic and copies ran while one was open for 54% of the time, Pallas kernels for 0%

profile of v1, /device:TPU:32, one launch (start us, length us, event | category | flops | bytes accessed | tf_op | source)
XLA Modules:
  0.0 380.6 jit_solution(18279140901157743070)
XLA Ops:
  7.2 19.9 %all_to_all.44 = bf16[128,32,2]{0,2,1:T(2,128)(2,1)S(1)} all-to-all(bf16[128,32,2]{0,2,1:T(2,128)(2,1)} %bitcast.128), channel_id=1, replica_groups=mesh['segment'=4,'ctx'=32,'tp'=2] {'ctx'}, dimensions={1} | all-to-all | bytes 32768 | tf_op jit(solution)/shard_map/all_to_all | solution.py:79
  27.1 2.4 stack.3
  29.5 5.9 %all-to-all-start = ((bf16[32,128,256]{2,1,0:T(8,128)(2,1)}), bf16[32,128,256]{2,1,0:T(8,128)(2,1)}, u32[]{:S(2)}, u32[]{:S(2)}) async-start(bf16[32,128,256]{2,1,0:T(8,128)(2,1)} %stack.3), calls=%async_computation | async-start | bytes 4194304 | tf_op jit(solution)/shard_map/all_to_all | solution.py:84
  38.4 2.9 copy.87
  43.7 44.3 %all-to-all-done = bf16[32,128,256]{2,1,0:T(8,128)(2,1)} async-done(((bf16[32,128,256]{2,1,0:T(8,128)(2,1)}), bf16[32,128,256]{2,1,0:T(8,128)(2,1)}, u32[]{:S(2)}, u32[]{:S(2)}) %all-to-all-start) | async-done | bytes 2097184 | tf_op jit(solution)/shard_map/all_to_all | solution.py:84
  88.0 6.2 %all-to-all-start.2 = ((bf16[128,32,128]{0,2,1:T(8,128)(2,1)}), bf16[128,32,128]{0,2,1:T(8,128)(2,1)S(1)}, u32[]{:S(2)}, u32[]{:S(2)}) async-start(bf16[128,32,128]{0,2,1:T(8,128)(2,1)} %bitcast.119), calls=%async_computation.2 | async-start | bytes 2097152 | tf_op jit(solution)/shard_map/all_to_all | solution.py:78
  101.5 3.3 copy.92
  105.2 3.0 fusion.54
  108.2 19.1 %all-to-all-done.2 = bf16[128,32,128]{0,2,1:T(8,128)(2,1)S(1)} async-done(((bf16[128,32,128]{0,2,1:T(8,128)(2,1)}), bf16[128,32,128]{0,2,1:T(8,128)(2,1)S(1)}, u32[]{:S(2)}, u32[]{:S(2)}) %all-to-all-start.2) | async-done | bytes 1048608 | tf_op jit(solution)/shard_map/all_to_all | solution.py:78
  127.3 2.4 fusion.36
  137.1 3.4 pad.35
  142.2 5.1 %pad.37 = f32[8,2,128,64]{2,3,1,0:T(8,128)} pad(f32[4,2,128,64]{2,3,1,0:T(8,128)} %add.123, f32[]{:T(128)} %constant.9.clone.1), padding=1_0_1x0_0_0x0_0_0x0_0_0 | pad | bytes 786436 | tf_op jit(solution)/shard_map/pad | solution.py:47
  148.4 3.2 pad.36
  156.0 9.2 %pad.38 = f32[16,2,128,64]{2,3,1,0:T(8,128)} pad(f32[8,2,128,64]{2,3,1,0:T(8,128)} %pad_maximum_fusion.1, f32[]{:T(128)} %constant.9.clone.1), padding=0_1_1x0_0_0x0_0_0x0_0_0 | pad | bytes 1572868 | tf_op jit(solution)/shard_map/pad | solution.py:47
  165.2 9.2 %pad.39 = f32[16,2,128,64]{2,3,1,0:T(8,128)} pad(f32[8,2,128,64]{2,3,1,0:T(8,128)} %add.125, f32[]{:T(128)} %constant.9.clone.1), padding=1_0_1x0_0_0x0_0_0x0_0_0 | pad | bytes 1572868 | tf_op jit(solution)/shard_map/pad | solution.py:47
  174.4 2.7 add.127
  177.1 16.5 %pad.73 = f32[32,2,128,64]{2,3,1,0:T(8,128)} pad(f32[16,2,128,64]{2,3,1,0:T(8,128)} %add.127, f32[]{:T(128)} %constant.9.clone.1), padding=1_0_1x0_0_0x0_0_0x0_0_0 | pad | bytes 3145732
  196.4 12.4 %pad.51 = f32[31,2,128,64]{2,3,1,0:T(8,128)S(1)} pad(f32[16,2,128,64]{2,3,1,0:T(8,128)} %pad_maximum_fusion, f32[]{:T(128)} %constant.9.clone.1), padding=0_0_1x0_0_0x0_0_0x0_0_0 | pad | bytes 3080196 | tf_op jit(solution)/shard_map/slice | solution.py:48
  208.8 2.4 fusion.62
  211.2 4.9 %fusion.6 = f32[32,2,128,64]{2,3,1,0:T(8,128)S(1)} fusion(bf16[32,128,2,64]{1,3,2,0:T(8,128)(2,1)S(1)} %bitcast.107, f32[32,128,2]{1,2,0:T(2,128)S(1)} %copy-done.11, f32[32,128,2]{1,2,0:T(2,128)S(1)} %copy-done.10, f32[32,128,128]{2,1,0:T(8,128)S(1)} %fusion.62, pred[128,128]{1,0:T(8,128)(4,1)S(1)} %copy-done.13), kind=kOutput, calls=%fused_computation.7 | convolution fusion | flops 810549248 | bytes 5324800 | tf_op jit(solution)/shard_map/cijh,cjhp->cihp/dot_general | solution.py:43
  216.2 3.3 fusion.15
  219.5 5.0 %all-to-all-start.3 = ((bf16[32,128,128]{1,2,0:T(8,128)(2,1)}), bf16[32,128,128]{1,2,0:T(8,128)(2,1)S(1)}, u32[]{:S(2)}, u32[]{:S(2)}) async-start(bf16[32,128,128]{1,2,0:T(8,128)(2,1)} %bitcast.116), calls=%async_computation.3 | async-start | bytes 2097152 | tf_op jit(solution)/shard_map/all_to_all | solution.py:90
  231.2 18.6 %all-to-all-done.3 = bf16[32,128,128]{1,2,0:T(8,128)(2,1)S(1)} async-done(((bf16[32,128,128]{1,2,0:T(8,128)(2,1)}), bf16[32,128,128]{1,2,0:T(8,128)(2,1)S(1)}, u32[]{:S(2)}, u32[]{:S(2)}) %all-to-all-start.3) | async-done | bytes 1048608 | tf_op jit(solution)/shard_map/all_to_all | solution.py:90
  251.4 2.9 copy.118
  254.3 2.4 fusion.24
  256.7 2.5 psum.7
  259.1 2.6 fusion.31
  263.4 26.5 %fusion.2 = (f32[4,8,128]{2,1,0:T(8,128)S(1)}, f32[4,4096,128,8]{2,1,3,0:T(8,128)}) fusion(pred[128,4096]{0,1:T(8,128)(4,1)S(1)} %fusion.32, bf16[4096,4,128,1]{0,2,3,1:T(8,128)(2,1)} %bitcast.117, bf16[128,4,8,128]{3,2,1,0:T(8,128)(2,1)S(1)} %bitcast.115), kind=kOutput, calls=%fused_computation.4 | convolution fusion | flops 4345294848 | bytes 72892416 | tf_op jit(solution)/shard_map/tkgd,skd->kgts/dot_general | solution.py:113
  290.0 21.8 %fusion = f32[4,8,128]{2,1,0:T(8,128)S(1)} fusion(f32[4,4096,128,8]{2,1,3,0:T(8,128)} %get-tuple-element.17, f32[4,8,128]{2,1,0:T(8,128)S(1)} %broadcast_maximum_fusion, pred[128,4096]{0,1:T(8,128)(4,1)S(1)} %fusion.32), kind=kLoop, calls=%fused_computation.2 | loop fusion | flops 67104768 | bytes 67665920 | tf_op jit(solution)/shard_map/reduce_sum | solution.py:121
  311.8 6.4 %copy.109 = bf16[1,4096,512]{1,2,0:T(8,128)(2,1)} copy(bf16[1,4096,512]{2,1,0:T(8,128)(2,1)} %all-gather.7.cloned.1.call-done) | data formatting | bytes 8388608 | tf_op jit(solution)/shard_map/all_gather | solution.py:106
  318.2 25.5 %fusion.16 = bf16[128,4,8,128]{0,3,2,1:T(8,128)(2,1)S(1)} fusion(bf16[4096,4,128,1]{0,2,3,1:T(8,128)(2,1)} %bitcast.118, f32[4,4096,128,8]{2,1,3,0:T(8,128)} %get-tuple-element.17, f32[4,8,128]{2,1,0:T(8,128)S(1)} %broadcast_maximum_fusion, pred[128,4096]{0,1:T(8,128)(4,1)S(1)} %fusion.32, f32[128,4,8]{0,2,1:T(8,128)S(1)} %bitcast.129), kind=kOutput, calls=%fused_computation.20 | convolution fusion | flops 4363124736 | bytes 72908800 | tf_op jit(solution)/shard_map/kgts,skd->kgtd/dot_general | solution.py:122
  345.6 24.9 %collective-permute-done.1 = bf16[128,4096]{1,0:T(8,128)(2,1)S(1)} collective-permute-done((bf16[128,4096]{1,0:T(8,128)(2,1)S(1)}, bf16[128,4096]{1,0:T(8,128)(2,1)S(1)}, u32[]{:S(2)}, u32[]{:S(2)}) %collective-permute-start.1) | collective-permute-done | bytes 1048608 | tf_op jit(solution)/shard_map/ppermute | solution.py:20
  (117 shorter events, 44.7 us)
Async XLA Ops:
  29.5 6.0 %copy-start.9 = (bf16[1,128,512]{2,1,0:T(8,128)(2,1)S(1)}, bf16[1,128,512]{2,1,0:T(8,128)(2,1)}, u32[]{:S(2)}) copy-start(bf16[1,128,512]{2,1,0:T(8,128)(2,1)} %param.19) | copy-start | bytes 393220
  29.5 6.8 %copy-start.5 = (bf16[1,128,4096]{2,1,0:T(8,128)(2,1)S(1)}, bf16[1,128,4096]{2,1,0:T(8,128)(2,1)}, u32[]{:S(2)}) copy-start(bf16[1,128,4096]{2,1,0:T(8,128)(2,1)} %param.11) | copy-start | bytes 3145732
  29.5 58.5 %all-to-all-start = ((bf16[32,128,256]{2,1,0:T(8,128)(2,1)}), bf16[32,128,256]{2,1,0:T(8,128)(2,1)}, u32[]{:S(2)}, u32[]{:S(2)}) async-start(bf16[32,128,256]{2,1,0:T(8,128)(2,1)} %stack.3), calls=%async_computation | async-start | bytes 4194304 | tf_op jit(solution)/shard_map/all_to_all | solution.py:84
  35.3 2.2 copy-start.14
  35.4 2.3 copy-start.15
  35.4 228.0 %all-gather.5.cloned.1.call-start = ((), (), s32[]{:S(2)}) async-start(), calls=%async_computation.4 | async-start | bytes 4325376 | tf_op jit(solution)/shard_map/all_gather | solution.py:105
  88.0 39.3 %all-to-all-start.2 = ((bf16[128,32,128]{0,2,1:T(8,128)(2,1)}), bf16[128,32,128]{0,2,1:T(8,128)(2,1)S(1)}, u32[]{:S(2)}, u32[]{:S(2)}) async-start(bf16[128,32,128]{0,2,1:T(8,128)(2,1)} %bitcast.119), calls=%async_computation.2 | async-start | bytes 2097152 | tf_op jit(solution)/shard_map/all_to_all | solution.py:78
  130.5 1.0 copy-start.2
  131.6 0.8 copy-start.4
  132.7 0.6 copy-start.6
  132.7 15.7 %slice-start.1 = ((f32[8,2,128,64]{2,3,1,0:T(8,128)}), f32[1,2,128,64]{2,3,1,0:T(8,128)S(1)}, s32[]{:S(2)}) async-start(f32[8,2,128,64]{2,3,1,0:T(8,128)} %copy-done.4), calls=%async_computation.7 | async-start | bytes 131072 | tf_op jit(solution)/shard_map/slice | solution.py:47
  148.4 6.7 %slice-start = ((f32[16,2,128,64]{2,3,1,0:T(8,128)}), f32[1,2,128,64]{2,3,1,0:T(8,128)S(1)}, s32[]{:S(2)}) async-start(f32[16,2,128,64]{2,3,1,0:T(8,128)} %copy-done.2), calls=%async_computation.6 | async-start | bytes 131072 | tf_op jit(solution)/shard_map/slice | solution.py:47
  193.6 1.7 copy-start.7
  208.7 2.4 copy-start.10
  208.7 2.4 copy-start.11
  208.8 2.4 copy-start.13
  211.2 5.0 %copy-start = (f32[32,2,128,64]{2,3,1,0:T(8,128)S(1)}, f32[32,2,128,64]{2,3,1,0:T(8,128)}, u32[]{:S(2)}) copy-start(f32[32,2,128,64]{2,3,1,0:T(8,128)} %pad.73) | copy-start | bytes 6291460
  211.2 5.0 %copy-start.1 = (bf16[4096,128]{1,0:T(8,128)(2,1)S(1)}, bf16[4096,128]{1,0:T(8,128)(2,1)}, u32[]{:S(2)}) copy-start(bf16[4096,128]{1,0:T(8,128)(2,1)} %get-tuple-element.3) | copy-start | bytes 3145732
  211.2 5.0 %copy-start.8 = (f32[32,128,2]{1,2,0:T(2,128)S(1)}, f32[32,128,2]{1,2,0:T(2,128)}, u32[]{:S(2)}) copy-start(f32[32,128,2]{1,2,0:T(2,128)} %copy.92) | copy-start | bytes 98308
  219.5 5.8 %copy-start.3 = (bf16[1,128,4096]{2,1,0:T(8,128)(2,1)S(1)}, bf16[1,128,4096]{2,1,0:T(8,128)(2,1)}, u32[]{:S(2)}) copy-start(bf16[1,128,4096]{2,1,0:T(8,128)(2,1)} %param.12) | copy-start | bytes 3145732
  219.5 30.3 %all-to-all-start.3 = ((bf16[32,128,128]{1,2,0:T(8,128)(2,1)}), bf16[32,128,128]{1,2,0:T(8,128)(2,1)S(1)}, u32[]{:S(2)}, u32[]{:S(2)}) async-start(bf16[32,128,128]{1,2,0:T(8,128)(2,1)} %bitcast.116), calls=%async_computation.3 | async-start | bytes 2097152 | tf_op jit(solution)/shard_map/all_to_all | solution.py:90
  224.5 87.3 %all-gather.7.cloned.1.call-start = ((), (), s32[]{:S(2)}) async-start(), calls=%async_computation.5 | async-start | bytes 4325376 | tf_op jit(solution)/shard_map/all_gather | solution.py:106
  254.3 4.8 %copy-start.12 = (f32[4096]{0:T(1024)S(1)}, f32[4096]{0:T(1024)}, u32[]{:S(2)}) copy-start(f32[4096]{0:T(1024)} %param.17) | copy-start | bytes 49156
  261.7 83.8 %collective-permute-start = (bf16[128,4096]{1,0:T(8,128)(2,1)S(1)}, bf16[128,4096]{1,0:T(8,128)(2,1)}, u32[]{:S(2)}, u32[]{:S(2)}) collective-permute-start(bf16[128,4096]{1,0:T(8,128)(2,1)S(1)} %fusion.31), channel_id=1, source_target_pairs={{0,64},{64,128},{128,192},{192,0},{1,65},{65,129},{129,193},{193,1... | collective-permute-start | bytes 3145736 | tf_op jit(solution)/shard_map/ppermute | solution.py:20
  344.2 26.3 %collective-permute-start.1 = (bf16[128,4096]{1,0:T(8,128)(2,1)S(1)}, bf16[128,4096]{1,0:T(8,128)(2,1)S(1)}, u32[]{:S(2)}, u32[]{:S(2)}) collective-permute-start(bf16[128,4096]{1,0:T(8,128)(2,1)S(1)} %copy.111), channel_id=1, source_target_pairs={{0,64},{64,128},{128,192},{192,0},{1,65},{65,129},{129,193},{193,1... | collective-permute-start | bytes 3145736 | tf_op jit(solution)/shard_map/ppermute | solution.py:20
Sparse Core Ops, SparseCore 0:
  38.7 109.0 all-gather.4
  228.0 83.1 all-gather.6
